TPU v7x, 32 devices: a whole 2x2x4 slice. The times are simulated.
32 devices in a mesh: dp: 16 (over z, y, x), tensor: 2 (over core).
Axes of the slice: x: 2, y: 2, z: 4, core: 2. Of those that a mesh axis runs over, the one named last changes fastest.
Arguments:
- tokens_in: bfloat16 [4096, 1536], P('dp'), may hold values from -6 to 6
- seq_lengths: int32 [16, 16], P('dp'), may hold values from 0 to 256, as said below
- gain_attn: bfloat16 [1536], P('dp'), may hold values from 0.099609375 to 1.8984375
- w_query: bfloat16 [1536, 1536], P(('tensor', 'dp')), may hold values from -3 to 3
- b_query: bfloat16 [1536], P(('tensor', 'dp')), may hold values from -3 to 3
- w_key: bfloat16 [256, 1536], P(('tensor', 'dp')), may hold values from -3 to 3
- b_key: bfloat16 [256], P(('tensor', 'dp')), may hold values from -3 to 3
- w_value: bfloat16 [256, 1536], P(('tensor', 'dp')), may hold values from -0.15625 to 0.15625
- b_value: bfloat16 [256], P(('tensor', 'dp')), may hold values from -3 to 3
- w_out: bfloat16 [1536, 1536], P(('tensor', 'dp')), may hold values from -0.625 to 0.625
- gain_mlp: bfloat16 [1536], P('dp'), may hold values from 0.099609375 to 1.8984375
- w_gate: bfloat16 [8960, 1536], P(('tensor', 'dp')), may hold values from -0.15625 to 0.15625
- w_up: bfloat16 [8960, 1536], P(('tensor', 'dp')), may hold values from -0.15625 to 0.15625
- w_down: bfloat16 [8960, 1536], P(('tensor', 'dp')), may hold values from -0.125 to 0.125
- grad_out: bfloat16 [4096, 1536], P('dp'), may hold values from -6 to 6
Outputs:
- block_out: float32 [4096, 1536], P('dp')
- grad_in: float32 [4096, 1536], P('dp')
- grad_gain_attn: float32 [1536], P('dp')
- grad_w_query: float32 [1536, 1536], P(('tensor', 'dp'))
- grad_b_query: float32 [1536], P(('tensor', 'dp'))
- grad_w_key: float32 [256, 1536], P(('tensor', 'dp'))
- grad_b_key: float32 [256], P('tensor')
- grad_w_value: float32 [256, 1536], P(('tensor', 'dp'))
- grad_b_value: float32 [256], P(('tensor', 'dp'))
- grad_w_out: float32 [1536, 1536], P(('tensor', 'dp'))
- grad_gain_mlp: float32 [1536], P('dp')
- grad_w_gate: float32 [8960, 1536], P(('tensor', 'dp'))
- grad_w_up: float32 [8960, 1536], P(('tensor', 'dp'))
- grad_w_down: float32 [8960, 1536], P(('tensor', 'dp'))
Inputs may be any that keep to these rules, and one draw needn't show every extreme that they name: `seq_lengths`: row r lists, in order, the lengths of the sequences packed in tokens r * 256 to (r + 1) * 256 - 1: they sum to 256, live slots come first and are 1 or more, unused slots are 0, and some row holds a single sequence of 256 tokens.
All inputs are finite; a program needn't handle non-finite values.
Results may differ from a plain program's by a relative error of at most 0.023.
Values may be sent and summed in bfloat16 or wider, within the bound.
No kernel may reach another device: no remote copies, remote signals or barrier semaphores. Data moves between devices by JAX's collectives and lax.ppermute only.
A program may use at most 256 MiB of HBM per device.

v0:
```python
import math
import jax
import jax.numpy as jnp
from jax import lax
from jax.sharding import PartitionSpec as P

H = 12
KVH = 2
HD = 128
EPSILON = 1e-06
ROPE_BASE = 1000000.0
BLOCK_LIMIT = 512


def packed_layout(seq_lengths, row_tokens):
    ends_all = jnp.cumsum(seq_lengths, axis=1)
    places = jnp.arange(row_tokens, dtype=jnp.int32)
    passed = ends_all[:, None, :] <= places[None, :, None]
    segment = jnp.sum(passed.astype(jnp.int32), axis=2)
    opening = jnp.sum(jnp.where(passed, seq_lengths[:, None, :], 0), axis=2)
    return (segment, places[None, :] - opening)


def rope_tables(positions):
    half_size = HD // 2
    frequency = ROPE_BASE ** (-(jnp.arange(half_size, dtype=jnp.float32) * 2.0) / HD)
    angles = positions.astype(jnp.float32)[:, None] * frequency[None, :]
    cosine = jnp.cos(angles)
    sine_table = jnp.sin(angles)
    return (
        jnp.concatenate([cosine, cosine], axis=1),
        jnp.concatenate([sine_table, sine_table], axis=1),
    )


def rotate(vectors, cosine, sine_table):
    half_size = vectors.shape[-1] // 2
    turned = jnp.concatenate([-vectors[..., half_size:], vectors[..., :half_size]], axis=-1)
    return vectors * cosine[:, None, :] + turned * sine_table[:, None, :]


def unrotate(gradient, cosine, sine_table):
    half_size = gradient.shape[-1] // 2
    scaled = gradient * sine_table[:, None, :]
    turned = jnp.concatenate([scaled[..., half_size:], -scaled[..., :half_size]], axis=-1)
    return gradient * cosine[:, None, :] + turned


def inverse_rms(values):
    return lax.rsqrt(jnp.mean(values * values, axis=1, keepdims=True) + EPSILON)


def project(left_side, weight):
    return jnp.einsum("td,fd->tf", left_side, weight, preferred_element_type=jnp.float32)


def contract(left_side, right_side):
    return lax.dot_general(
        left_side, right_side, (((0,), (0,)), ((), ())), preferred_element_type=jnp.float32
    )


def masked_scores(query_block, keys_rot, allowed, score_scale):
    scores = (
        jnp.einsum("qkgd,tkd->kgqt", query_block, keys_rot, preferred_element_type=jnp.float32)
        * score_scale
    )
    return jnp.where(allowed[None, None], scores, -jnp.inf)


def shards(
    tokens_in,
    seq_lengths,
    gain_attn,
    w_query,
    b_query,
    w_key,
    b_key,
    w_value,
    b_value,
    w_out,
    gain_mlp,
    w_gate,
    w_up,
    w_down,
    grad_out,
):
    row_tokens = tokens_in.shape[0]
    group_heads = H // KVH
    score_scale = 1.0 / math.sqrt(HD)
    segments, positions = packed_layout(seq_lengths, row_tokens)
    segment = segments[0]
    cosine, sine_table = rope_tables(positions[0])
    places = jnp.arange(row_tokens, dtype=jnp.int32)
    block_rows = min(row_tokens, BLOCK_LIMIT)
    block_count = row_tokens // block_rows
    segment_blocks = segment.reshape(block_count, block_rows)
    place_blocks = places.reshape(block_count, block_rows)

    def block_mask(segment_block, place_block):
        return (segment_block[:, None] == segment[None, :]) & (
            place_block[:, None] >= places[None, :]
        )

    gathered = (
        lax.all_gather(gain_attn, "dp", axis=0, tiled=True),
        lax.all_gather(w_query, "dp", axis=0, tiled=True),
        lax.all_gather(b_query, "dp", axis=0, tiled=True),
        lax.all_gather(w_key, "dp", axis=0, tiled=True),
        lax.all_gather(b_key, "dp", axis=0, tiled=True),
        lax.all_gather(w_value, "dp", axis=0, tiled=True),
        lax.all_gather(b_value, "dp", axis=0, tiled=True),
        lax.all_gather(w_out, "dp", axis=0, tiled=True),
        lax.all_gather(gain_mlp, "dp", axis=0, tiled=True),
    )
    (
        gain_first,
        query_weight,
        query_bias,
        key_weight,
        key_bias,
        value_weight,
        value_bias,
        out_weight,
        gain_second,
    ) = gathered
    query_heads = query_weight.shape[0] // HD
    key_heads = key_weight.shape[0] // HD
    inputs = tokens_in.astype(jnp.float32)
    inverse_first = inverse_rms(inputs)
    normed_first = inputs * inverse_first
    first_low = (normed_first * gain_first.astype(jnp.float32)).astype(jnp.bfloat16)
    query_pre = project(first_low, query_weight) + query_bias.astype(jnp.float32)
    keys_pre = project(first_low, key_weight) + key_bias.astype(jnp.float32)
    values_pre = project(first_low, value_weight) + value_bias.astype(jnp.float32)
    query_rot = rotate(query_pre.reshape(row_tokens, query_heads, HD), cosine, sine_table).astype(
        jnp.bfloat16
    )
    keys_rot = rotate(keys_pre.reshape(row_tokens, key_heads, HD), cosine, sine_table).astype(
        jnp.bfloat16
    )
    values_low = values_pre.reshape(row_tokens, key_heads, HD).astype(jnp.bfloat16)
    query_blocks = query_rot.reshape(block_count, block_rows, key_heads, group_heads, HD)

    def forward_block(operands):
        query_block, segment_block, place_block = operands
        scores = masked_scores(
            query_block, keys_rot, block_mask(segment_block, place_block), score_scale
        )
        largest = jnp.max(scores, axis=3, keepdims=True)
        log_total = largest + jnp.log(jnp.sum(jnp.exp(scores - largest), axis=3, keepdims=True))
        probability = jnp.exp(scores - log_total).astype(jnp.bfloat16)
        attended_block = jnp.einsum(
            "kgqt,tkd->qkgd", probability, values_low, preferred_element_type=jnp.float32
        )
        return (attended_block.astype(jnp.bfloat16), log_total)

    attended_blocks, log_totals = lax.map(
        forward_block, (query_blocks, segment_blocks, place_blocks)
    )
    attended = attended_blocks.reshape(row_tokens, query_heads * HD)
    attn_part = jnp.dot(attended, out_weight, preferred_element_type=jnp.float32)
    hidden_state = inputs + lax.psum(attn_part, "tensor")
    inverse_second = inverse_rms(hidden_state)
    normed_second = hidden_state * inverse_second
    second_low = (normed_second * gain_second.astype(jnp.float32)).astype(jnp.bfloat16)
    piece_gate = lax.all_gather(w_gate, "dp", axis=0, tiled=True)
    piece_up = lax.all_gather(w_up, "dp", axis=0, tiled=True)
    piece_down = lax.all_gather(w_down, "dp", axis=0, tiled=True)
    gate_vals = project(second_low, piece_gate)
    up_vals = project(second_low, piece_up)
    hidden_low = (jax.nn.silu(gate_vals) * up_vals).astype(jnp.bfloat16)
    mlp_part = jnp.dot(hidden_low, piece_down, preferred_element_type=jnp.float32)
    block_out = hidden_state + lax.psum(mlp_part.astype(jnp.bfloat16), "tensor").astype(jnp.float32)
    piece_gate = lax.all_gather(w_gate, "dp", axis=0, tiled=True)
    piece_up = lax.all_gather(w_up, "dp", axis=0, tiled=True)
    piece_down = lax.all_gather(w_down, "dp", axis=0, tiled=True)
    gate_vals = project(second_low, piece_gate)
    up_vals = project(second_low, piece_up)
    sigmoid_vals = jax.nn.sigmoid(gate_vals)
    silu_vals = jax.nn.silu(gate_vals)
    hidden_low = (silu_vals * up_vals).astype(jnp.bfloat16)
    grad_hidden = project(grad_out, piece_down)
    grad_gate = (
        grad_hidden * up_vals * (sigmoid_vals * (1.0 + gate_vals * (1.0 - sigmoid_vals)))
    ).astype(jnp.bfloat16)
    grad_up = (grad_hidden * silu_vals).astype(jnp.bfloat16)
    grad_second = jnp.dot(grad_gate, piece_gate, preferred_element_type=jnp.float32) + jnp.dot(
        grad_up, piece_up, preferred_element_type=jnp.float32
    )
    gate_grads = grad_gate
    up_grads = grad_up
    hidden_all = hidden_low
    grad_second, gate_grads, up_grads, hidden_all = (grad_second, gate_grads, up_grads, hidden_all)
    grad_second = lax.psum(grad_second, "tensor")
    traded = (
        lax.all_to_all(gate_grads, "dp", split_axis=1, concat_axis=0, tiled=True),
        lax.all_to_all(up_grads, "dp", split_axis=1, concat_axis=0, tiled=True),
        lax.all_to_all(hidden_all, "dp", split_axis=1, concat_axis=0, tiled=True),
    )
    piece_second = lax.all_gather(second_low, "dp", axis=0, tiled=True)
    piece_grad = lax.all_gather(grad_out, "dp", axis=0, tiled=True)
    gate_rows = traded[0]
    up_rows = traded[1]
    hidden_rows = traded[2]
    grad_w_gate = contract(gate_rows, piece_second)
    grad_w_up = contract(up_rows, piece_second)
    grad_w_down = contract(hidden_rows, piece_grad)
    grad_gain_second = jnp.sum(grad_second * normed_second, axis=0)
    scaled_second = grad_second * gain_second.astype(jnp.float32)
    grad_hidden_state = grad_out.astype(jnp.float32) + inverse_second * (
        scaled_second
        - normed_second * jnp.mean(scaled_second * normed_second, axis=1, keepdims=True)
    )
    grad_branch = grad_hidden_state.astype(jnp.bfloat16)
    back_first, back_query, back_key, back_value, back_out = (
        lax.all_gather(gain_attn, "dp", axis=0, tiled=True),
        lax.all_gather(w_query, "dp", axis=0, tiled=True),
        lax.all_gather(w_key, "dp", axis=0, tiled=True),
        lax.all_gather(w_value, "dp", axis=0, tiled=True),
        lax.all_gather(w_out, "dp", axis=0, tiled=True),
    )
    grad_out_weight = contract(attended, grad_branch)
    grad_attended = project(grad_branch, back_out).astype(jnp.bfloat16)
    grad_blocks = grad_attended.reshape(block_count, block_rows, key_heads, group_heads, HD)

    def backward_block(operands):
        query_block, segment_block, place_block, log_total, grad_block = operands
        scores = masked_scores(
            query_block, keys_rot, block_mask(segment_block, place_block), score_scale
        )
        probability = jnp.exp(scores - log_total)
        grad_prob = jnp.einsum(
            "qkgd,tkd->kgqt", grad_block, values_low, preferred_element_type=jnp.float32
        )
        weighted = jnp.sum(probability * grad_prob, axis=3, keepdims=True)
        grad_scores = (probability * (grad_prob - weighted)).astype(jnp.bfloat16)
        grad_query = (
            jnp.einsum("kgqt,tkd->qkgd", grad_scores, keys_rot, preferred_element_type=jnp.float32)
            * score_scale
        )
        grad_keys = (
            jnp.einsum(
                "kgqt,qkgd->tkd", grad_scores, query_block, preferred_element_type=jnp.float32
            )
            * score_scale
        )
        grad_values = jnp.einsum(
            "kgqt,qkgd->tkd",
            probability.astype(jnp.bfloat16),
            grad_block,
            preferred_element_type=jnp.float32,
        )
        return (grad_query, grad_keys, grad_values)

    query_parts, key_parts, value_parts = lax.map(
        backward_block, (query_blocks, segment_blocks, place_blocks, log_totals, grad_blocks)
    )
    grad_query_low = (
        unrotate(query_parts.reshape(row_tokens, query_heads, HD), cosine, sine_table)
        .reshape(row_tokens, query_heads * HD)
        .astype(jnp.bfloat16)
    )
    grad_keys_low = (
        unrotate(jnp.sum(key_parts, axis=0), cosine, sine_table)
        .reshape(row_tokens, key_heads * HD)
        .astype(jnp.bfloat16)
    )
    grad_values_low = (
        jnp.sum(value_parts, axis=0).reshape(row_tokens, key_heads * HD).astype(jnp.bfloat16)
    )
    grad_query_weight = contract(grad_query_low, first_low)
    grad_query_bias = jnp.sum(grad_query_low, axis=0, dtype=jnp.float32)
    grad_key_weight = contract(grad_keys_low, first_low)
    grad_key_bias = jnp.sum(grad_keys_low, axis=0, dtype=jnp.float32)
    grad_value_weight = contract(grad_values_low, first_low)
    grad_value_bias = jnp.sum(grad_values_low, axis=0, dtype=jnp.float32)
    key_bias_total = lax.psum(grad_key_bias, "dp")
    grad_first = jnp.dot(grad_query_low, back_query, preferred_element_type=jnp.float32)
    grad_first = grad_first + jnp.dot(grad_keys_low, back_key, preferred_element_type=jnp.float32)
    grad_first = grad_first + jnp.dot(
        grad_values_low, back_value, preferred_element_type=jnp.float32
    )
    grad_first = lax.psum(grad_first.astype(jnp.bfloat16), "tensor").astype(jnp.float32)
    grad_gain_first = jnp.sum(grad_first * normed_first, axis=0)
    scaled_first = grad_first * back_first.astype(jnp.float32)
    grad_in = grad_hidden_state + inverse_first * (
        scaled_first - normed_first * jnp.mean(scaled_first * normed_first, axis=1, keepdims=True)
    )
    summed = (
        lax.psum_scatter(grad_gain_first, "dp", scatter_dimension=0, tiled=True),
        lax.psum_scatter(grad_query_weight, "dp", scatter_dimension=0, tiled=True),
        lax.psum_scatter(grad_query_bias, "dp", scatter_dimension=0, tiled=True),
        lax.psum_scatter(grad_key_weight, "dp", scatter_dimension=0, tiled=True),
        lax.psum_scatter(grad_value_weight, "dp", scatter_dimension=0, tiled=True),
        lax.psum_scatter(grad_value_bias, "dp", scatter_dimension=0, tiled=True),
        lax.psum_scatter(grad_out_weight, "dp", scatter_dimension=0, tiled=True),
        lax.psum_scatter(grad_gain_second, "dp", scatter_dimension=0, tiled=True),
    )
    return (
        block_out,
        grad_in,
        summed[0],
        summed[1],
        summed[2],
        summed[3],
        key_bias_total,
        summed[4],
        summed[5],
        summed[6],
        summed[7],
        grad_w_gate,
        grad_w_up,
        grad_w_down,
    )


def solution(mesh):
    in_specs = (
        P("dp", None),
        P("dp", None),
        P("dp"),
        P(("tensor", "dp"), None),
        P(("tensor", "dp")),
        P(("tensor", "dp"), None),
        P(("tensor", "dp")),
        P(("tensor", "dp"), None),
        P(("tensor", "dp")),
        P(("tensor", "dp"), None),
        P("dp"),
        P(("tensor", "dp"), None),
        P(("tensor", "dp"), None),
        P(("tensor", "dp"), None),
        P("dp", None),
    )
    out_specs = (
        P("dp", None),
        P("dp", None),
        P("dp"),
        P(("tensor", "dp"), None),
        P(("tensor", "dp")),
        P(("tensor", "dp"), None),
        P("tensor"),
        P(("tensor", "dp"), None),
        P(("tensor", "dp")),
        P(("tensor", "dp"), None),
        P("dp"),
        P(("tensor", "dp"), None),
        P(("tensor", "dp"), None),
        P(("tensor", "dp"), None),
    )
    return jax.shard_map(shards, mesh=mesh, in_specs=in_specs, out_specs=out_specs, check_vma=False)
```

profile of v0, /device:TPU:0, one launch (start us, length us, event | category | flops | bytes accessed | tf_op | source)
XLA Modules:
  0.0 1759.0 jit_solution(16797219213902656720)
XLA Ops:
  17.9 79.2 %all-reduce.10 = (bf16[128]{0:T(256)(128)(2,1)S(1)}, bf16[1536]{0:T(1024)(128)(2,1)S(1)}, bf16[128]{0:T(256)(128)(2,1)S(1)}, bf16[768]{0:T(1024)(128)(2,1)S(1)}, bf16[1536]{0:T(1024)(128)(2,1)}) all-reduce(bf16[128]{0:T(256)(128)(2,1)S(1)} %dynamic-update-slice.1, ...), channel_id=1, replica_groups=mesh['dp'=16,'tensor'=2] {'dp'}, use_global_device_ids=true, to_apply=%add.1 | all-reduce | flops 4096 | bytes 16384
  98.5 39.9 %all_gather.53 = bf16[128,1536]{1,0:T(8,128)(2,1)S(1)} all-gather(bf16[8,1536]{1,0:T(8,128)(2,1)} %param.20), channel_id=1, replica_groups=mesh['dp'=16,'tensor'=2] {'dp'}, dimensions={0}, use_global_device_ids=true | all-gather | bytes 417792 | tf_op jit(solution)/shard_map/all_gather | solution.py:109
  140.9 39.7 %all_gather.51 = bf16[128,1536]{1,0:T(8,128)(2,1)S(1)} all-gather(bf16[8,1536]{1,0:T(8,128)(2,1)S(1)} %copy-done.36), channel_id=1, replica_groups=mesh['dp'=16,'tensor'=2] {'dp'}, dimensions={0}, use_global_device_ids=true | all-gather | bytes 417792 | tf_op jit(solution)/shard_map/all_gather | solution.py:111
  195.7 13.5 all-reduce.16.cloned.1.call-done
  212.7 162.9 %all-gather.12.cloned.1.call-done = bf16[4480,1536]{1,0:T(8,128)(2,1)} async-done(((bf16[280,1536]{1,0:T(8,128)(2,1)}), bf16[4480,1536]{1,0:T(8,128)(2,1)}) %all-gather.12.cloned.1.call-update) | async-done | bytes 13762576 | tf_op jit(solution)/shard_map/all_gather | solution.py:167
  375.6 11.1 fusion.58
  386.7 152.3 %all-gather.14.cloned.1.call-done = bf16[4480,1536]{1,0:T(8,128)(2,1)} async-done(((bf16[280,1536]{1,0:T(8,128)(2,1)}), bf16[4480,1536]{1,0:T(8,128)(2,1)}) %all-gather.14.cloned.1.call-update) | async-done | bytes 13762576 | tf_op jit(solution)/shard_map/all_gather | solution.py:168
  539.0 11.1 fusion.59
  550.1 152.3 %all-gather.16.cloned.1.call-done = bf16[4480,1536]{1,0:T(8,128)(2,1)} async-done(((bf16[280,1536]{1,0:T(8,128)(2,1)}), bf16[4480,1536]{1,0:T(8,128)(2,1)}) %all-gather.16.cloned.1.call-update) | async-done | bytes 13762576 | tf_op jit(solution)/shard_map/all_gather | solution.py:169
  702.4 11.3 multiply_convert_fusion
  713.7 8.7 fusion.60
  732.8 11.1 convolution_convert_fusion
  791.8 59.0 %all-to-all-done = bf16[256,16,280]{0,2,1:T(8,128)(2,1)} async-done(((bf16[256,16,280]{0,2,1:T(8,128)(2,1)}), bf16[256,16,280]{0,2,1:T(8,128)(2,1)}, u32[]{:S(2)}, u32[]{:S(2)}) %all-to-all-start) | async-done | bytes 2293792 | tf_op jit(solution)/shard_map/all_to_all | solution.py:197
  850.8 22.3 %all-to-all-start.1 = ((bf16[256,16,280]{0,2,1:T(8,128)(2,1)}), bf16[256,16,280]{0,2,1:T(8,128)(2,1)}, u32[]{:S(2)}, u32[]{:S(2)}) async-start(bf16[256,16,280]{0,2,1:T(8,128)(2,1)} %bitcast.157), calls=%async_computation.5 | async-start | bytes 4587520 | tf_op jit(solution)/shard_map/all_to_all | solution.py:198
  881.7 51.8 %all-to-all-done.1 = bf16[256,16,280]{0,2,1:T(8,128)(2,1)} async-done(((bf16[256,16,280]{0,2,1:T(8,128)(2,1)}), bf16[256,16,280]{0,2,1:T(8,128)(2,1)}, u32[]{:S(2)}, u32[]{:S(2)}) %all-to-all-start.1) | async-done | bytes 2293792 | tf_op jit(solution)/shard_map/all_to_all | solution.py:198
  933.4 37.2 %all-to-all-start.2 = ((bf16[256,16,280]{0,2,1:T(8,128)(2,1)}), bf16[256,16,280]{0,2,1:T(8,128)(2,1)}, u32[]{:S(2)}, u32[]{:S(2)}) async-start(bf16[256,16,280]{0,2,1:T(8,128)(2,1)} %bitcast.156), calls=%async_computation.6 | async-start | bytes 4587520 | tf_op jit(solution)/shard_map/all_to_all | solution.py:199
  974.5 138.6 %all-reduce.9 = (f32[1536]{0:T(1024)S(1)}, f32[768]{0:T(1024)S(1)}, f32[128]{0:T(128)}, f32[128]{0:T(128)S(1)}, f32[1536]{0:T(1024)S(1)}) all-reduce(f32[1536]{0:T(1024)S(1)} %get-tuple-element.67, f32[768]{0:T(1024)S(1)} %bitcast.172, f32[128]{0:T(128)S(1)} %copy-done.43, ...), channel_id=2, replica_groups=mesh['dp'=16,'tensor'=2] {'dp'}, use_global_device_ids=true, to_apply=%region_15.16.clone | all-reduce | flops 4096 | bytes 32768
  1127.9 10.3 fusion.62
  1143.2 67.4 %all-gather.20.cloned.1.call-done = bf16[4096,1536]{1,0:T(8,128)(2,1)} async-done(((bf16[256,1536]{1,0:T(8,128)(2,1)}), bf16[4096,1536]{1,0:T(8,128)(2,1)}) %all-gather.20.cloned.1.call-update) | async-done | bytes 12582928 | tf_op jit(solution)/shard_map/all_gather | solution.py:202
  1210.6 10.2 fusion.64
  1220.8 117.2 %reduce-scatter.7.cloned.1.call-done = f32[8,1536]{1,0:T(8,128)} async-done(((f32[128,1536]{1,0:T(8,128)}), f32[8,1536]{1,0:T(8,128)}) %reduce-scatter.7.cloned.1.call-update) | async-done | bytes 49168 | tf_op jit(solution)/shard_map/reduce_scatter | solution.py:294
  1338.0 128.0 %reduce-scatter.9.cloned.1.call-done = f32[8,1536]{1,0:T(8,128)} async-done(((f32[128,1536]{1,0:T(8,128)}), f32[8,1536]{1,0:T(8,128)}) %reduce-scatter.9.cloned.1.call-update) | async-done | bytes 49168 | tf_op jit(solution)/shard_map/reduce_scatter | solution.py:295
  1466.0 143.4 %reduce-scatter.5.cloned.1.call-done = f32[48,1536]{1,0:T(8,128)} async-done(((f32[768,1536]{1,0:T(8,128)}), f32[48,1536]{1,0:T(8,128)}) %reduce-scatter.5.cloned.1.call-update) | async-done | bytes 294928 | tf_op jit(solution)/shard_map/reduce_scatter | solution.py:292
  1609.4 142.8 %reduce-scatter.11.cloned.1.call-done = f32[48,1536]{1,0:T(8,128)} async-done(((f32[768,1536]{1,0:T(8,128)}), f32[48,1536]{1,0:T(8,128)}) %reduce-scatter.11.cloned.1.call-update) | async-done | bytes 294928 | tf_op jit(solution)/shard_map/reduce_scatter | solution.py:297
  (210 shorter events, 119.0 us)
Async XLA Ops:
  7.2 131.5 %copy-start = (bf16[256,1536]{1,0:T(8,128)(2,1)S(1)}, bf16[256,1536]{1,0:T(8,128)(2,1)}, u32[]{:S(2)}) copy-start(bf16[256,1536]{1,0:T(8,128)(2,1)} %param.15) | copy-start | bytes 2359300
  7.2 175.2 %all-gather.8.cloned.1.call-start = ((), (), s32[]{:S(2)}) async-start(), calls=%async_computation.7 | async-start | bytes 2506752 | tf_op jit(solution)/shard_map/all_gather | solution.py:107
  7.9 181.2 %all-gather.10.cloned.1.call-start = ((), (), s32[]{:S(2)}) async-start(), calls=%async_computation.8 | async-start | bytes 2506752 | tf_op jit(solution)/shard_map/all_gather | solution.py:113
  8.7 200.5 %all-reduce.16.cloned.1.call-start = ((), (), s32[]{:S(2)}) async-start(), calls=%async_computation.9 | async-start | bytes 3145728 | tf_op jit(solution)/shard_map/psum | solution.py:163
  10.4 128.8 %copy-start.41 = (f32[64]{0:T(128)}, f32[64]{0:T(128)S(1)}, u32[]{:S(2)}) copy-start(f32[64]{0:T(128)S(1)} %multiply_power_fusion) | copy-start | bytes 772
  138.4 44.0 %copy-start.33 = (f32[256]{0:T(256)}, f32[256]{0:T(256)S(1)}, u32[]{:S(2)}) copy-start(f32[256]{0:T(256)S(1)} %add_rsqrt_fusion.1) | copy-start | bytes 3076
  139.9 45.4 %copy-start.21 = (f32[256,128]{0,1:T(8,128)}, f32[256,128]{0,1:T(8,128)S(1)}, u32[]{:S(2)}) copy-start(f32[256,128]{0,1:T(8,128)S(1)} %get-tuple-element.114) | copy-start | bytes 393220
  192.8 182.8 %all-gather.12.cloned.1.call-start = ((), (), s32[]{:S(2)}) async-start(), calls=%async_computation.10 | async-start | bytes 14622720 | tf_op jit(solution)/shard_map/all_gather | solution.py:167
  193.4 345.6 %all-gather.14.cloned.1.call-start = ((), (), s32[]{:S(2)}) async-start(), calls=%async_computation.11 | async-start | bytes 14622720 | tf_op jit(solution)/shard_map/all_gather | solution.py:168
  194.0 508.5 %all-gather.16.cloned.1.call-start = ((), (), s32[]{:S(2)}) async-start(), calls=%async_computation.12 | async-start | bytes 14622720 | tf_op jit(solution)/shard_map/all_gather | solution.py:169
  194.5 555.1 %all-reduce.18.cloned.1.call-start = ((), (), s32[]{:S(2)}) async-start(), calls=%async_computation.13 | async-start | bytes 3145728 | tf_op jit(solution)/shard_map/psum | solution.py:195
  713.7 8.8 copy-start.15
  730.9 241.7 %all-reduce.20.cloned.1.call-start = ((), (), s32[]{:S(2)}) async-start(), calls=%async_computation.20 | async-start | bytes 3145728 | tf_op jit(solution)/shard_map/psum | solution.py:174
  768.9 359.0 %all-gather.18.cloned.1.call-start = ((), (), s32[]{:S(2)}) async-start(), calls=%async_computation.18 | async-start | bytes 13369344 | tf_op jit(solution)/shard_map/all_gather | solution.py:201
  769.7 440.9 %all-gather.20.cloned.1.call-start = ((), (), s32[]{:S(2)}) async-start(), calls=%async_computation.19 | async-start | bytes 13369344 | tf_op jit(solution)/shard_map/all_gather | solution.py:202
  770.2 567.7 %reduce-scatter.7.cloned.1.call-start = ((), (), s32[]{:S(2)}) async-start(), calls=%async_computation.15 | async-start | bytes 835584 | tf_op jit(solution)/shard_map/reduce_scatter | solution.py:294
  771.7 694.4 %reduce-scatter.9.cloned.1.call-start = ((), (), s32[]{:S(2)}) async-start(), calls=%async_computation.16 | async-start | bytes 835584 | tf_op jit(solution)/shard_map/reduce_scatter | solution.py:295
  773.1 836.3 %reduce-scatter.5.cloned.1.call-start = ((), (), s32[]{:S(2)}) async-start(), calls=%async_computation.14 | async-start | bytes 5013504 | tf_op jit(solution)/shard_map/reduce_scatter | solution.py:292
  780.6 70.2 %all-to-all-start = ((bf16[256,16,280]{0,2,1:T(8,128)(2,1)}), bf16[256,16,280]{0,2,1:T(8,128)(2,1)}, u32[]{:S(2)}, u32[]{:S(2)}) async-start(bf16[256,16,280]{0,2,1:T(8,128)(2,1)} %bitcast.158), calls=%async_computation.4 | async-start | bytes 4587520 | tf_op jit(solution)/shard_map/all_to_all | solution.py:197
  850.8 82.7 %all-to-all-start.1 = ((bf16[256,16,280]{0,2,1:T(8,128)(2,1)}), bf16[256,16,280]{0,2,1:T(8,128)(2,1)}, u32[]{:S(2)}, u32[]{:S(2)}) async-start(bf16[256,16,280]{0,2,1:T(8,128)(2,1)} %bitcast.157), calls=%async_computation.5 | async-start | bytes 4587520 | tf_op jit(solution)/shard_map/all_to_all | solution.py:198
  873.0 879.2 %reduce-scatter.11.cloned.1.call-start = ((), (), s32[]{:S(2)}) async-start(), calls=%async_computation.17 | async-start | bytes 5013504 | tf_op jit(solution)/shard_map/reduce_scatter | solution.py:297
  933.4 191.1 %all-to-all-start.2 = ((bf16[256,16,280]{0,2,1:T(8,128)(2,1)}), bf16[256,16,280]{0,2,1:T(8,128)(2,1)}, u32[]{:S(2)}, u32[]{:S(2)}) async-start(bf16[256,16,280]{0,2,1:T(8,128)(2,1)} %bitcast.156), calls=%async_computation.6 | async-start | bytes 4587520 | tf_op jit(solution)/shard_map/all_to_all | solution.py:199
  972.6 142.8 %copy-start.13 = (bf16[256,1536]{1,0:T(8,128)(2,1)S(1)}, bf16[256,1536]{1,0:T(8,128)(2,1)}, u32[]{:S(2)}) copy-start(bf16[256,1536]{1,0:T(8,128)(2,1)} %get-tuple-element.94) | copy-start | bytes 2359300
  1127.9 10.3 copy-start.44
  (38 other events, 78.4 us)
Sparse Core Ops, SparseCore 0:
  10.8 65.3 all-gather.7
  79.0 64.5 all-gather.9
  192.9 16.2 all-reduce.15
  211.8 163.7 all-gather.11
  378.2 160.7 all-gather.13
  541.7 160.7 all-gather.15
  731.1 18.5 all-reduce.17
  769.0 21.6 all-reduce.19
  794.1 261.4 all-gather.17
  1058.2 152.3 all-gather.19
  1215.9 122.0 reduce-scatter.6
  1343.1 122.8 reduce-scatter.8
  1471.8 137.5 reduce-scatter.4
  1615.0 137.1 reduce-scatter.10
where the time goes:
time: 1770 us; the launch traced here: 1760 us
  waiting for transfers between devices  1200 us (68%)
  blocking collectives  297 us (17%)
  matrix products  114 us (6%)
  starting transfers between devices  67.4 us (4%)
  local copies, waits for them, and re-layouts  41.1 us (2%)
  other arithmetic  19.8 us (1%)
  between operations  18.7 us (1%)
    unnamed x2, blocking collectives  218 us
    all_gather x1, waiting for transfers between devices, shards(): piece_gate = lax.all_gather(w_gate, 'dp', axis=0, tiled=True)  163 us
    all_gather x1, waiting for transfers between devices, shards(): piece_up = lax.all_gather(w_up, 'dp', axis=0, tiled=True)  152 us
    all_gather x1, waiting for transfers between devices, shards(): piece_down = lax.all_gather(w_down, 'dp', axis=0, tiled=True)  152 us
    reduce_scatter x1, waiting for transfers between devices, shards(): lax.psum_scatter(grad_query_weight, 'dp', scatter_dimension=0, tiled=True)  143 us
    reduce_scatter x1, waiting for transfers between devices, shards(): lax.psum_scatter(grad_out_weight, 'dp', scatter_dimension=0, tiled=True)  143 us
    reduce_scatter x1, waiting for transfers between devices, shards(): lax.psum_scatter(grad_value_weight, 'dp', scatter_dimension=0, tiled=True)  128 us
    reduce_scatter x1, waiting for transfers between devices, shards(): lax.psum_scatter(grad_key_weight, 'dp', scatter_dimension=0, tiled=True)  117 us
  transfers between devices with their start and end apart: 17, of which 12 were waited for; matrix products, arithmetic and copies ran while one was open for 7% of the time, Pallas kernels for 0%

commit v1 on v0

--- a/solution.py
+++ b/solution.py
@@ -193,10 +193,23 @@
     hidden_all = hidden_low
     grad_second, gate_grads, up_grads, hidden_all = (grad_second, gate_grads, up_grads, hidden_all)
     grad_second = lax.psum(grad_second, "tensor")
+
+    def show_the_slabs(vector, named_axis, where_dim, which_dim):
+        prior = jnp.concatenate(
+            lax.all_to_all(
+                jnp.stack(jnp.split(vector, lax.axis_size(named_axis), axis=where_dim)),
+                axis_name=named_axis,
+                split_axis=0,
+                concat_axis=0,
+            ),
+            which_dim,
+        )
+        return prior
+
     traded = (
         lax.all_to_all(gate_grads, "dp", split_axis=1, concat_axis=0, tiled=True),
         lax.all_to_all(up_grads, "dp", split_axis=1, concat_axis=0, tiled=True),
-        lax.all_to_all(hidden_all, "dp", split_axis=1, concat_axis=0, tiled=True),
+        show_the_slabs(hidden_all, "dp", 1, 0),
     )
     piece_second = lax.all_gather(second_low, "dp", axis=0, tiled=True)
     piece_grad = lax.all_gather(grad_out, "dp", axis=0, tiled=True)

time: 1770 us -> 1770 us (level)
  waiting for transfers between devices: 1200 us -> 1170 us
  local copies, waits for them, and re-layouts: 41.1 us -> 70.6 us
    all_to_all x1, waiting for transfers between devices: 51.8 us -> 24.7 us  [shards(): lax.all_to_all(up_grads, 'dp', split_axis=1, concat_axis=0, tiled=True)]
    unnamed x105 -> x120, local copies, waits for them, and re-layouts: 15.8 us -> 41.1 us
  transfers between devices with their start and end apart: 17 -> 17, of which waited for: 12 -> 12; matrix products, arithmetic and copies ran while one was open for 7% -> 9% of each run, Pallas kernels for 0% -> 0%
where the time goes in v1:
time: 1770 us; the launch traced here: 1760 us
  waiting for transfers between devices  1170 us (66%)
  blocking collectives  298 us (17%)
  matrix products  114 us (6%)
  local copies, waits for them, and re-layouts  70.6 us (4%)
  starting transfers between devices  67.3 us (4%)
  other arithmetic  20.5 us (1%)
  between operations  18.7 us (1%)
    unnamed x2, blocking collectives  218 us
    all_gather x1, waiting for transfers between devices, shards(): piece_gate = lax.all_gather(w_gate, 'dp', axis=0, tiled=True)  163 us
    all_gather x1, waiting for transfers between devices, shards(): piece_up = lax.all_gather(w_up, 'dp', axis=0, tiled=True)  152 us
    all_gather x1, waiting for transfers between devices, shards(): piece_down = lax.all_gather(w_down, 'dp', axis=0, tiled=True)  152 us
    reduce_scatter x1, waiting for transfers between devices, shards(): lax.psum_scatter(grad_query_weight, 'dp', scatter_dimension=0, tiled=True)  144 us
    reduce_scatter x1, waiting for transfers between devices, shards(): lax.psum_scatter(grad_out_weight, 'dp', scatter_dimension=0, tiled=True)  143 us
    reduce_scatter x1, waiting for transfers between devices, shards(): lax.psum_scatter(grad_value_weight, 'dp', scatter_dimension=0, tiled=True)  128 us
    reduce_scatter x1, waiting for transfers between devices, shards(): lax.psum_scatter(grad_key_weight, 'dp', scatter_dimension=0, tiled=True)  117 us
  transfers between devices with their start and end apart: 17, of which 12 were waited for; matrix products, arithmetic and copies ran while one was open for 9% of the time, Pallas kernels for 0%

profile of v1, /device:TPU:0, one launch (start us, length us, event | category | flops | bytes accessed | tf_op | source)
XLA Modules:
  0.0 1760.5 jit_solution(16412283652838006506)
XLA Ops:
  17.9 79.2 %all-reduce.10 = (bf16[128]{0:T(256)(128)(2,1)S(1)}, bf16[1536]{0:T(1024)(128)(2,1)S(1)}, bf16[128]{0:T(256)(128)(2,1)S(1)}, bf16[768]{0:T(1024)(128)(2,1)S(1)}, bf16[1536]{0:T(1024)(128)(2,1)}) all-reduce(bf16[128]{0:T(256)(128)(2,1)S(1)} %dynamic-update-slice.1, ...), channel_id=1, replica_groups=mesh['dp'=16,'tensor'=2] {'dp'}, use_global_device_ids=true, to_apply=%add.1 | all-reduce | flops 4096 | bytes 16384
  98.5 39.6 %all_gather.53 = bf16[128,1536]{1,0:T(8,128)(2,1)S(1)} all-gather(bf16[8,1536]{1,0:T(8,128)(2,1)} %param.20), channel_id=1, replica_groups=mesh['dp'=16,'tensor'=2] {'dp'}, dimensions={0}, use_global_device_ids=true | all-gather | bytes 417792 | tf_op jit(solution)/shard_map/all_gather | solution.py:109
  141.5 40.0 %all_gather.51 = bf16[128,1536]{1,0:T(8,128)(2,1)S(1)} all-gather(bf16[8,1536]{1,0:T(8,128)(2,1)S(1)} %copy-done.37), channel_id=1, replica_groups=mesh['dp'=16,'tensor'=2] {'dp'}, dimensions={0}, use_global_device_ids=true | all-gather | bytes 417792 | tf_op jit(solution)/shard_map/all_gather | solution.py:111
  197.4 13.5 all-reduce.16.cloned.1.call-done
  214.5 162.9 %all-gather.12.cloned.1.call-done = bf16[4480,1536]{1,0:T(8,128)(2,1)} async-done(((bf16[280,1536]{1,0:T(8,128)(2,1)}), bf16[4480,1536]{1,0:T(8,128)(2,1)}) %all-gather.12.cloned.1.call-update) | async-done | bytes 13762576 | tf_op jit(solution)/shard_map/all_gather | solution.py:167
  377.3 11.1 fusion.74
  388.4 152.3 %all-gather.14.cloned.1.call-done = bf16[4480,1536]{1,0:T(8,128)(2,1)} async-done(((bf16[280,1536]{1,0:T(8,128)(2,1)}), bf16[4480,1536]{1,0:T(8,128)(2,1)}) %all-gather.14.cloned.1.call-update) | async-done | bytes 13762576 | tf_op jit(solution)/shard_map/all_gather | solution.py:168
  540.8 11.1 fusion.75
  551.9 152.3 %all-gather.16.cloned.1.call-done = bf16[4480,1536]{1,0:T(8,128)(2,1)} async-done(((bf16[280,1536]{1,0:T(8,128)(2,1)}), bf16[4480,1536]{1,0:T(8,128)(2,1)}) %all-gather.16.cloned.1.call-update) | async-done | bytes 13762576 | tf_op jit(solution)/shard_map/all_gather | solution.py:169
  704.2 11.3 multiply_convert_fusion
  715.5 8.7 fusion.76
  734.5 11.1 convolution_convert_fusion
  792.3 59.0 %all-to-all-done = bf16[256,16,280]{0,2,1:T(8,128)(2,1)} async-done(((bf16[256,16,280]{0,2,1:T(8,128)(2,1)}), bf16[256,16,280]{0,2,1:T(8,128)(2,1)}, u32[]{:S(2)}, u32[]{:S(2)}) %all-to-all-start) | async-done | bytes 2293792 | tf_op jit(solution)/shard_map/all_to_all | solution.py:210
  851.4 22.3 %all-to-all-start.1 = ((bf16[256,16,280]{0,2,1:T(8,128)(2,1)}), bf16[256,16,280]{0,2,1:T(8,128)(2,1)}, u32[]{:S(2)}, u32[]{:S(2)}) async-start(bf16[256,16,280]{0,2,1:T(8,128)(2,1)} %bitcast.218), calls=%async_computation.5 | async-start | bytes 4587520 | tf_op jit(solution)/shard_map/all_to_all | solution.py:211
  909.4 24.7 %all-to-all-done.1 = bf16[256,16,280]{0,2,1:T(8,128)(2,1)} async-done(((bf16[256,16,280]{0,2,1:T(8,128)(2,1)}), bf16[256,16,280]{0,2,1:T(8,128)(2,1)}, u32[]{:S(2)}, u32[]{:S(2)}) %all-to-all-start.1) | async-done | bytes 2293792 | tf_op jit(solution)/shard_map/all_to_all | solution.py:211
  934.0 36.7 %all-to-all-start.2 = ((bf16[16,256,280]{1,2,0:T(8,128)(2,1)}), bf16[16,256,280]{1,2,0:T(8,128)(2,1)}, u32[]{:S(2)}, u32[]{:S(2)}) async-start(bf16[16,256,280]{1,2,0:T(8,128)(2,1)} %copy.121), calls=%async_computation.6 | async-start | bytes 4587520 | tf_op jit(solution)/shard_map/all_to_all | solution.py:199
  974.6 139.1 %all-reduce.9 = (f32[1536]{0:T(1024)S(1)}, f32[768]{0:T(1024)S(1)}, f32[128]{0:T(128)}, f32[128]{0:T(128)S(1)}, f32[1536]{0:T(1024)S(1)}) all-reduce(f32[1536]{0:T(1024)S(1)} %get-tuple-element.67, f32[768]{0:T(1024)S(1)} %bitcast.233, f32[128]{0:T(128)S(1)} %get-tuple-element.95, ...), channel_id=2, replica_groups=mesh['dp'=16,'tensor'=2] {'dp'}, use_global_device_ids=true, to_apply=%region_15.16.clone | all-reduce | flops 4096 | bytes 32768
  1130.0 10.3 fusion.78
  1146.5 64.7 %all-gather.20.cloned.1.call-done = bf16[4096,1536]{1,0:T(8,128)(2,1)} async-done(((bf16[256,1536]{1,0:T(8,128)(2,1)}), bf16[4096,1536]{1,0:T(8,128)(2,1)}) %all-gather.20.cloned.1.call-update) | async-done | bytes 12582928 | tf_op jit(solution)/shard_map/all_gather | solution.py:215
  1211.2 10.2 fusion.80
  1221.4 117.2 %reduce-scatter.7.cloned.1.call-done = f32[8,1536]{1,0:T(8,128)} async-done(((f32[128,1536]{1,0:T(8,128)}), f32[8,1536]{1,0:T(8,128)}) %reduce-scatter.7.cloned.1.call-update) | async-done | bytes 49168 | tf_op jit(solution)/shard_map/reduce_scatter | solution.py:307
  1338.6 127.9 %reduce-scatter.9.cloned.1.call-done = f32[8,1536]{1,0:T(8,128)} async-done(((f32[128,1536]{1,0:T(8,128)}), f32[8,1536]{1,0:T(8,128)}) %reduce-scatter.9.cloned.1.call-update) | async-done | bytes 49168 | tf_op jit(solution)/shard_map/reduce_scatter | solution.py:308
  1466.5 144.1 %reduce-scatter.5.cloned.1.call-done = f32[48,1536]{1,0:T(8,128)} async-done(((f32[768,1536]{1,0:T(8,128)}), f32[48,1536]{1,0:T(8,128)}) %reduce-scatter.5.cloned.1.call-update) | async-done | bytes 294928 | tf_op jit(solution)/shard_map/reduce_scatter | solution.py:305
  1610.6 143.1 %reduce-scatter.11.cloned.1.call-done = f32[48,1536]{1,0:T(8,128)} async-done(((f32[768,1536]{1,0:T(8,128)}), f32[48,1536]{1,0:T(8,128)}) %reduce-scatter.11.cloned.1.call-update) | async-done | bytes 294928 | tf_op jit(solution)/shard_map/reduce_scatter | solution.py:310
  (226 shorter events, 149.2 us)
Async XLA Ops:
  7.2 176.1 %all-gather.8.cloned.1.call-start = ((), (), s32[]{:S(2)}) async-start(), calls=%async_computation.7 | async-start | bytes 2506752 | tf_op jit(solution)/shard_map/all_gather | solution.py:107
  7.9 183.0 %all-gather.10.cloned.1.call-start = ((), (), s32[]{:S(2)}) async-start(), calls=%async_computation.8 | async-start | bytes 2506752 | tf_op jit(solution)/shard_map/all_gather | solution.py:113
  8.7 202.3 %all-reduce.16.cloned.1.call-start = ((), (), s32[]{:S(2)}) async-start(), calls=%async_computation.9 | async-start | bytes 3145728 | tf_op jit(solution)/shard_map/psum | solution.py:163
  10.4 127.8 %copy-start.42 = (f32[64]{0:T(128)}, f32[64]{0:T(128)S(1)}, u32[]{:S(2)}) copy-start(f32[64]{0:T(128)S(1)} %multiply_power_fusion) | copy-start | bytes 772
  138.1 45.2 %copy-start.34 = (f32[256]{0:T(256)}, f32[256]{0:T(256)S(1)}, u32[]{:S(2)}) copy-start(f32[256]{0:T(256)S(1)} %add_rsqrt_fusion.1) | copy-start | bytes 3076
  140.5 41.0 %copy-start = (bf16[256,1536]{1,0:T(8,128)(2,1)S(1)}, bf16[256,1536]{1,0:T(8,128)(2,1)}, u32[]{:S(2)}) copy-start(bf16[256,1536]{1,0:T(8,128)(2,1)} %param.15) | copy-start | bytes 2359300
  141.2 41.4 %copy-start.11 = (f32[256,128]{0,1:T(8,128)}, f32[256,128]{0,1:T(8,128)S(1)}, u32[]{:S(2)}) copy-start(f32[256,128]{0,1:T(8,128)S(1)} %get-tuple-element.112) | copy-start | bytes 393220
  141.2 45.0 %copy-start.22 = (f32[256,128]{0,1:T(8,128)}, f32[256,128]{0,1:T(8,128)S(1)}, u32[]{:S(2)}) copy-start(f32[256,128]{0,1:T(8,128)S(1)} %get-tuple-element.114) | copy-start | bytes 393220
  194.5 182.8 %all-gather.12.cloned.1.call-start = ((), (), s32[]{:S(2)}) async-start(), calls=%async_computation.10 | async-start | bytes 14622720 | tf_op jit(solution)/shard_map/all_gather | solution.py:167
  195.1 345.7 %all-gather.14.cloned.1.call-start = ((), (), s32[]{:S(2)}) async-start(), calls=%async_computation.11 | async-start | bytes 14622720 | tf_op jit(solution)/shard_map/all_gather | solution.py:168
  195.7 508.5 %all-gather.16.cloned.1.call-start = ((), (), s32[]{:S(2)}) async-start(), calls=%async_computation.12 | async-start | bytes 14622720 | tf_op jit(solution)/shard_map/all_gather | solution.py:169
  196.3 555.1 %all-reduce.18.cloned.1.call-start = ((), (), s32[]{:S(2)}) async-start(), calls=%async_computation.13 | async-start | bytes 3145728 | tf_op jit(solution)/shard_map/psum | solution.py:195
  732.7 240.0 %all-reduce.20.cloned.1.call-start = ((), (), s32[]{:S(2)}) async-start(), calls=%async_computation.20 | async-start | bytes 3145728 | tf_op jit(solution)/shard_map/psum | solution.py:174
  769.5 360.6 %all-gather.18.cloned.1.call-start = ((), (), s32[]{:S(2)}) async-start(), calls=%async_computation.18 | async-start | bytes 13369344 | tf_op jit(solution)/shard_map/all_gather | solution.py:214
  770.2 441.0 %all-gather.20.cloned.1.call-start = ((), (), s32[]{:S(2)}) async-start(), calls=%async_computation.19 | async-start | bytes 13369344 | tf_op jit(solution)/shard_map/all_gather | solution.py:215
  770.8 567.8 %reduce-scatter.7.cloned.1.call-start = ((), (), s32[]{:S(2)}) async-start(), calls=%async_computation.15 | async-start | bytes 835584 | tf_op jit(solution)/shard_map/reduce_scatter | solution.py:307
  772.2 694.2 %reduce-scatter.9.cloned.1.call-start = ((), (), s32[]{:S(2)}) async-start(), calls=%async_computation.16 | async-start | bytes 835584 | tf_op jit(solution)/shard_map/reduce_scatter | solution.py:308
  773.7 836.9 %reduce-scatter.5.cloned.1.call-start = ((), (), s32[]{:S(2)}) async-start(), calls=%async_computation.14 | async-start | bytes 5013504 | tf_op jit(solution)/shard_map/reduce_scatter | solution.py:305
  781.1 70.2 %all-to-all-start = ((bf16[256,16,280]{0,2,1:T(8,128)(2,1)}), bf16[256,16,280]{0,2,1:T(8,128)(2,1)}, u32[]{:S(2)}, u32[]{:S(2)}) async-start(bf16[256,16,280]{0,2,1:T(8,128)(2,1)} %bitcast.219), calls=%async_computation.4 | async-start | bytes 4587520 | tf_op jit(solution)/shard_map/all_to_all | solution.py:210
  851.4 82.7 %all-to-all-start.1 = ((bf16[256,16,280]{0,2,1:T(8,128)(2,1)}), bf16[256,16,280]{0,2,1:T(8,128)(2,1)}, u32[]{:S(2)}, u32[]{:S(2)}) async-start(bf16[256,16,280]{0,2,1:T(8,128)(2,1)} %bitcast.218), calls=%async_computation.5 | async-start | bytes 4587520 | tf_op jit(solution)/shard_map/all_to_all | solution.py:211
  873.7 880.0 %reduce-scatter.11.cloned.1.call-start = ((), (), s32[]{:S(2)}) async-start(), calls=%async_computation.17 | async-start | bytes 5013504 | tf_op jit(solution)/shard_map/reduce_scatter | solution.py:310
  909.4 65.2 %copy-start.36 = (f32[1536]{0:T(1024)S(1)}, f32[1536]{0:T(1024)}, u32[]{:S(2)}) copy-start(f32[1536]{0:T(1024)} %get-tuple-element.65) | copy-start | bytes 18436
  909.4 65.2 %copy-start.43 = (f32[128]{0:T(128)S(1)}, f32[128]{0:T(128)}, u32[]{:S(2)}) copy-start(f32[128]{0:T(128)} %get-tuple-element.129) | copy-start | bytes 1540
  934.0 192.7 %all-to-all-start.2 = ((bf16[16,256,280]{1,2,0:T(8,128)(2,1)}), bf16[16,256,280]{1,2,0:T(8,128)(2,1)}, u32[]{:S(2)}, u32[]{:S(2)}) async-start(bf16[16,256,280]{1,2,0:T(8,128)(2,1)} %copy.121), calls=%async_computation.6 | async-start | bytes 4587520 | tf_op jit(solution)/shard_map/all_to_all | solution.py:199
  (38 other events, 119.8 us)
Sparse Core Ops, SparseCore 0:
  10.8 65.3 all-gather.7
  79.0 65.1 all-gather.9
  194.6 16.2 all-reduce.15
  213.6 163.7 all-gather.11
  380.0 160.7 all-gather.13
  543.4 160.7 all-gather.15
  732.8 18.5 all-reduce.17
  769.6 21.5 all-reduce.19
  794.6 261.4 all-gather.17
  1058.7 152.4 all-gather.19
  1216.5 122.0 reduce-scatter.6
  1343.7 122.7 reduce-scatter.8
  1472.2 138.3 reduce-scatter.4
  1616.2 137.4 reduce-scatter.10
